TPU v7x, 32 devices: a whole 2x2x4 slice. The times are simulated.
32 devices in a mesh: dp: 8 (over z, x), tensor: 4 (over y, core).
Axes of the slice: x: 2, y: 2, z: 4, core: 2. Of those that a mesh axis runs over, the one named last changes fastest.
Arguments:
- tokens: bfloat16 [24, 512, 768], P('dp', None, 'tensor'), may hold values from -6 to 6
- cotangent: bfloat16 [24, 512, 768], P('dp', None, 'tensor'), may hold values from -6 to 6
- prev_logits: bfloat16 [24, 12, 512, 512], P('dp', 'tensor'), may hold values from -6 to 6
- segment_ids: int32 [24, 512], P('dp'), may hold values from 0 to 5, never falling along the last dimension, each value on 1 to 256 neighbouring positions
- w_qkv: float32 [768, 3, 768], P('dp', None, 'tensor'), may hold values from -0.21875 to 0.21875
- b_qv: float32 [2, 768], P(None, 'tensor'), may hold values from -3 to 3
- w_out: float32 [768, 768], P('tensor', 'dp'), may hold values from -0.625 to 0.625
- w_up: float32 [768, 3072], P('dp', 'tensor'), may hold values from -0.21875 to 0.21875
- b_up: float32 [3072], P('tensor'), may hold values from -3 to 3
- w_down: float32 [3072, 768], P('tensor', 'dp'), may hold values from -0.109375 to 0.109375
- biases: float32 [2, 768], replicated, may hold values from -3 to 3
- gains: float32 [2, 768], replicated, may hold values from 0.25 to 1.75
- shifts: float32 [2, 768], replicated, may hold values from -3 to 3
Outputs:
- activations: bfloat16 [24, 512, 768], P('dp', None, 'tensor')
- raw_logits: bfloat16 [24, 12, 512, 512], P('dp', 'tensor')
- input_grad: bfloat16 [24, 512, 768], P('dp', None, 'tensor')
- logits_grad: bfloat16 [24, 12, 512, 512], P('dp', 'tensor')
- grad_qkv: float32 [768, 3, 768], P(None, None, 'tensor')
- grad_b_qv: float32 [2, 768], P(None, 'tensor')
- grad_out: float32 [768, 768], P('tensor')
- grad_up: float32 [768, 3072], P(None, 'tensor')
- grad_b_up: float32 [3072], P('tensor')
- grad_down: float32 [3072, 768], P('tensor')
- grad_biases: float32 [2, 768], replicated
- grad_gains: float32 [2, 768], replicated
- grad_shifts: float32 [2, 768], replicated
Inputs may be any that keep to these rules, and one draw needn't show every extreme that they name: `segment_ids`: in each row the segment number never falls; each segment has 1 to 256 slots and one has exactly that many; a query attends only to keys of its own segment.
All inputs are finite; a program needn't handle non-finite values.
Results may differ from a plain program's by a relative error of at most 0.02.
Values may be sent and summed in bfloat16 or wider, within the bound.
No kernel may reach another device: no remote copies, remote signals or barrier semaphores. Data moves between devices by JAX's collectives and lax.ppermute only.
A program may use at most 192 MiB of HBM per device.

v0:
```python
import math
import jax
import jax.numpy as jnp
from jax import lax
from jax.sharding import PartitionSpec as P

EPS = 1e-06
NEG = -1e30


def gelu_exact(values):
    return jax.nn.gelu(values, approximate=False)


def norm_forward(summed, gain_row, shift_row):
    row_mean = jnp.mean(summed, axis=-1, keepdims=True)
    centered = summed - row_mean
    inv_std = lax.rsqrt(jnp.mean(centered * centered, axis=-1, keepdims=True) + EPS)
    normed = centered * inv_std
    return (normed * gain_row + shift_row, normed, inv_std)


def norm_backward(grad_output, normed, inv_std, gain_row):
    scaled = grad_output * gain_row
    inner = (
        scaled
        - jnp.mean(scaled, axis=-1, keepdims=True)
        - normed * jnp.mean(scaled * normed, axis=-1, keepdims=True)
    )
    return inner * inv_std


def branch_total(partial_value):
    return lax.psum(partial_value.astype(jnp.bfloat16), "tensor").astype(jnp.float32)


def attend_rows(query, keys, values, previous, segment, inv_root):
    allowed = (segment[:, None] == segment[None, :])[None]
    scores = jnp.einsum(
        "qhe,khe->hqk", query, keys, preferred_element_type=jnp.float32
    ) * inv_root + previous.astype(jnp.float32)
    masked = jnp.where(allowed, scores, NEG)
    row_max = jnp.max(masked, axis=-1, keepdims=True)
    expanded = jnp.exp(masked - row_max)
    row_sum = jnp.sum(expanded, axis=-1, keepdims=True)
    probability = (expanded / row_sum).astype(jnp.bfloat16)
    output = jnp.einsum(
        "hqk,khe->qhe", probability, values, preferred_element_type=jnp.float32
    ).astype(jnp.bfloat16)
    log_total = row_max[..., 0] + jnp.log(row_sum[..., 0])
    return (output, scores.astype(jnp.bfloat16), log_total)


def attend_back(query, keys, values, previous, segment, log_total, grad_heads, inv_root):
    allowed = (segment[:, None] == segment[None, :])[None]
    scores = jnp.einsum(
        "qhe,khe->hqk", query, keys, preferred_element_type=jnp.float32
    ) * inv_root + previous.astype(jnp.float32)
    probability = jnp.where(allowed, jnp.exp(scores - log_total[..., None]), 0.0)
    grad_prob = jnp.einsum("qhe,khe->hqk", grad_heads, values, preferred_element_type=jnp.float32)
    grad_values = jnp.einsum(
        "hqk,qhe->khe",
        probability.astype(jnp.bfloat16),
        grad_heads,
        preferred_element_type=jnp.float32,
    )
    inner = jnp.sum(grad_prob * probability, axis=-1, keepdims=True)
    grad_scores = (probability * (grad_prob - inner)).astype(jnp.bfloat16)
    grad_query = (
        jnp.einsum("hqk,khe->qhe", grad_scores, keys, preferred_element_type=jnp.float32) * inv_root
    )
    grad_keys = (
        jnp.einsum("hqk,qhe->khe", grad_scores, query, preferred_element_type=jnp.float32)
        * inv_root
    )
    return (grad_query, grad_keys, grad_values, grad_scores)


def body(
    tokens,
    cotangent,
    prev_logits,
    segment_ids,
    w_qkv,
    b_qv,
    w_out,
    w_up,
    b_up,
    w_down,
    biases,
    gains,
    shifts,
):
    row_count, slot_count, part_width = tokens.shape
    full_width = part_width * lax.axis_size("tensor")
    local_width = b_qv.shape[1]
    heads_here = prev_logits.shape[1]
    head_size = local_width // heads_here
    token_count = row_count * slot_count
    inv_root = 1.0 / math.sqrt(head_size)
    my_cols = lax.axis_index("tensor") * part_width
    gathered_x, gathered_dy = (
        lax.all_gather(tokens, "tensor", axis=2, tiled=True),
        lax.all_gather(cotangent, "tensor", axis=2, tiled=True),
    )
    inputs_bf = gathered_x.reshape(token_count, full_width)
    grad_final = gathered_dy.reshape(token_count, full_width).astype(jnp.float32)
    qkv_weight, up_weight = (
        lax.all_gather(w_qkv.astype(jnp.bfloat16), "dp", axis=0, tiled=True),
        lax.all_gather(w_up.astype(jnp.bfloat16), "dp", axis=0, tiled=True),
    )
    out_weight, down_weight = (
        lax.all_gather(w_out.astype(jnp.bfloat16), "dp", axis=1, tiled=True),
        lax.all_gather(w_down.astype(jnp.bfloat16), "dp", axis=1, tiled=True),
    )
    qkv_matrix = qkv_weight.reshape(full_width, 3 * local_width)
    qkv_bias = jnp.stack([b_qv[0], jnp.zeros_like(b_qv[0]), b_qv[1]])

    def project(source, matrix):
        product = jnp.dot(source, matrix, preferred_element_type=jnp.float32).reshape(
            token_count, 3, local_width
        )
        return (
            (product + qkv_bias)
            .astype(jnp.bfloat16)
            .reshape(row_count, slot_count, 3, heads_here, head_size)
        )

    def attend_all(packed):

        def one_row(row_items):
            return attend_rows(
                row_items[0], row_items[1], row_items[2], row_items[3], row_items[4], inv_root
            )

        return lax.map(
            one_row, (packed[:, :, 0], packed[:, :, 1], packed[:, :, 2], prev_logits, segment_ids)
        )

    qkv_all = project(inputs_bf, qkv_matrix)
    attn_heads, raw_scores, log_total = attend_all(qkv_all)
    attn_flat = attn_heads.reshape(token_count, local_width)
    attn_partial = jnp.dot(attn_flat, out_weight, preferred_element_type=jnp.float32)
    first_out, normed_one, inv_one = norm_forward(
        inputs_bf.astype(jnp.float32) + branch_total(attn_partial) + biases[0], gains[0], shifts[0]
    )
    first_bf = first_out.astype(jnp.bfloat16)
    hidden = jnp.dot(first_bf, up_weight, preferred_element_type=jnp.float32) + b_up
    activated = gelu_exact(hidden).astype(jnp.bfloat16)
    ffn_partial = jnp.dot(activated, down_weight, preferred_element_type=jnp.float32)
    final_out, normed_two, inv_two = norm_forward(
        first_out + branch_total(ffn_partial) + biases[1], gains[1], shifts[1]
    )
    block_out = (
        lax.dynamic_slice_in_dim(final_out, my_cols, part_width, 1)
        .reshape(row_count, slot_count, part_width)
        .astype(jnp.bfloat16)
    )
    grad_gain_two = jnp.sum(grad_final * normed_two, axis=0)
    grad_shift_two = jnp.sum(grad_final, axis=0)
    grad_sum_two = norm_backward(grad_final, normed_two, inv_two, gains[1])
    grad_bias_down = jnp.sum(grad_sum_two, axis=0)
    grad_sum_two_bf = grad_sum_two.astype(jnp.bfloat16)
    again = lax.optimization_barrier((inputs_bf, qkv_matrix, first_bf, up_weight, grad_sum_two_bf))
    qkv_back = project(again[0], again[1])
    attn_back = attend_all(qkv_back)[0].reshape(token_count, local_width)
    first_back = again[2]
    hidden_back = jnp.dot(first_back, again[3], preferred_element_type=jnp.float32) + b_up
    act_back = gelu_exact(hidden_back).astype(jnp.bfloat16)
    grad_down = jnp.dot(act_back.T, grad_sum_two_bf, preferred_element_type=jnp.float32)
    grad_act = jnp.dot(grad_sum_two_bf, down_weight.T, preferred_element_type=jnp.float32)
    grad_hidden = jax.vjp(gelu_exact, hidden_back)[1](grad_act)[0]
    grad_bias_up = jnp.sum(grad_hidden, axis=0)
    grad_hidden_bf = grad_hidden.astype(jnp.bfloat16)
    grad_up = jnp.dot(first_back.T, grad_hidden_bf, preferred_element_type=jnp.float32)
    ffn_summed = (grad_up, grad_bias_up, grad_down, grad_bias_down, grad_gain_two, grad_shift_two)
    first_partial = jnp.dot(grad_hidden_bf, up_weight.T, preferred_element_type=jnp.float32)
    grad_first = grad_sum_two + branch_total(first_partial)
    grad_gain_one = jnp.sum(grad_first * normed_one, axis=0)
    grad_shift_one = jnp.sum(grad_first, axis=0)
    grad_sum_one = norm_backward(grad_first, normed_one, inv_one, gains[0])
    grad_bias_out = jnp.sum(grad_sum_one, axis=0)
    grad_sum_one_bf = grad_sum_one.astype(jnp.bfloat16)
    own_grad = lax.dynamic_slice_in_dim(grad_sum_one, my_cols, part_width, 1)
    grad_out = jnp.dot(attn_back.T, grad_sum_one_bf, preferred_element_type=jnp.float32)
    grad_heads = jnp.dot(grad_sum_one_bf, out_weight.T, preferred_element_type=jnp.float32).astype(
        jnp.bfloat16
    )
    grad_heads = grad_heads.reshape(row_count, slot_count, heads_here, head_size)

    def back_row(row_items):
        return attend_back(
            row_items[0],
            row_items[1],
            row_items[2],
            row_items[3],
            row_items[4],
            row_items[5],
            row_items[6],
            inv_root,
        )

    grad_query, grad_keys, grad_values, grad_scores = lax.map(
        back_row,
        (
            qkv_back[:, :, 0],
            qkv_back[:, :, 1],
            qkv_back[:, :, 2],
            prev_logits,
            segment_ids,
            log_total,
            grad_heads,
        ),
    )
    grad_qkv_full = jnp.stack([grad_query, grad_keys, grad_values], axis=2).reshape(
        token_count, 3, local_width
    )
    grad_b_qv = jnp.stack(
        [jnp.sum(grad_qkv_full[:, 0], axis=0), jnp.sum(grad_qkv_full[:, 2], axis=0)]
    )
    grad_qkv_bf = grad_qkv_full.reshape(token_count, 3 * local_width).astype(jnp.bfloat16)
    grad_qkv = jnp.dot(inputs_bf.T, grad_qkv_bf, preferred_element_type=jnp.float32).reshape(
        full_width, 3, local_width
    )
    grad_input_part = jnp.dot(grad_qkv_bf, qkv_matrix.T, preferred_element_type=jnp.float32)
    grad_input = (
        lax.psum_scatter(
            grad_input_part.astype(jnp.bfloat16), "tensor", scatter_dimension=1, tiled=True
        ).astype(jnp.float32)
        + own_grad
    )
    grad_input = grad_input.reshape(row_count, slot_count, part_width).astype(jnp.bfloat16)
    every_sum = lax.psum(
        (
            grad_qkv,
            grad_b_qv,
            grad_out,
            grad_bias_out,
            grad_gain_one,
            grad_shift_one,
            ffn_summed[0],
            ffn_summed[1],
            ffn_summed[2],
            ffn_summed[3],
            ffn_summed[4],
            ffn_summed[5],
        ),
        "dp",
    )
    attn_summed = every_sum[:6]
    ffn_final = every_sum[6:]
    grad_biases_all = jnp.stack([attn_summed[3], ffn_final[3]])
    grad_gains_all = jnp.stack([attn_summed[4], ffn_final[4]])
    grad_shifts_all = jnp.stack([attn_summed[5], ffn_final[5]])
    return (
        block_out,
        raw_scores,
        grad_input,
        grad_scores,
        attn_summed[0],
        attn_summed[1],
        attn_summed[2],
        ffn_final[0],
        ffn_final[1],
        ffn_final[2],
        grad_biases_all,
        grad_gains_all,
        grad_shifts_all,
    )


def solution(mesh):
    placed = (
        P("dp", None, "tensor"),
        P("dp", None, "tensor"),
        P("dp", "tensor", None, None),
        P("dp", None),
        P("dp", None, "tensor"),
        P(None, "tensor"),
        P("tensor", "dp"),
        P("dp", "tensor"),
        P("tensor"),
        P("tensor", "dp"),
        P(),
        P(),
        P(),
    )
    return jax.shard_map(
        body,
        mesh=mesh,
        in_specs=placed,
        out_specs=(
            P("dp", None, "tensor"),
            P("dp", "tensor", None, None),
            P("dp", None, "tensor"),
            P("dp", "tensor", None, None),
            P(None, None, "tensor"),
            P(None, "tensor"),
            P("tensor", None),
            P(None, "tensor"),
            P("tensor"),
            P("tensor", None),
            P(),
            P(),
            P(),
        ),
        check_vma=False,
    )
```

profile of v0, /device:TPU:0, one launch (start us, length us, event | category | flops | bytes accessed | tf_op | source)
XLA Modules:
  0.0 772.9 jit_solution(10725266084257419247)
XLA Ops:
  10.9 38.8 %all_gather.19 = bf16[768,3,192]{2,1,0:T(4,128)(2,1)S(1)} all-gather(bf16[96,3,192]{2,1,0:T(4,128)(2,1)S(1)} %copy.112), channel_id=1, replica_groups=mesh['dp'=8,'tensor'=4] {'dp'}, dimensions={0}, use_global_device_ids=true | all-gather | bytes 995328 | tf_op jit(solution)/shard_map/all_gather | solution.py:109
  50.7 7.0 copy.117
  57.7 33.0 %all_gather.20 = bf16[192,768]{0,1:T(8,128)(2,1)} all-gather(bf16[192,96]{0,1:T(8,128)(2,1)S(1)} %copy.119), channel_id=1, replica_groups=mesh['dp'=8,'tensor'=4] {'dp'}, dimensions={1}, use_global_device_ids=true | all-gather | bytes 331776 | tf_op jit(solution)/shard_map/all_gather | solution.py:113
  90.7 2.8 copy.111
  93.6 2.8 add_convert_fusion.1
  96.4 5.2 reshape.263
  101.5 2.7 slice_bitcast_fusion.3
  108.9 40.5 %while.40 = (s32[]{:T(128)}, bf16[3,512,3,64]{1,3,2,0:T(8,128)(2,1)}, bf16[3,3,512,512]{3,2,1,0:T(8,128)(2,1)}, f32[3,3,512]{2,1,0:T(4,128)}, bf16[3,512,3,64]{1...) while((s32[]{:T(128)}, ...), condition=%wide.region_3.4_spmd, body=%wide.region_0.3_spmd.sunk | while | flops 211909120 | bytes 20769400 | solution.py:136
  119.8 2.7 constant_dynamic-update-slice_fusion.4
  151.3 3.2 convolution_convert_fusion.3
  157.6 52.0 %all-reduce.7.cloned.1.call-done = bf16[1536,768]{1,0:T(8,128)(2,1)} async-done(((bf16[1536,768]{1,0:T(8,128)(2,1)}), bf16[1536,768]{1,0:T(8,128)(2,1)}) %all-reduce.7.cloned.1.call-update) | async-done | bytes 2359312 | tf_op jit(solution)/shard_map/psum | solution.py:34
  213.6 2.7 fusion.110
  216.3 24.9 %all-gather.9.cloned.1.call-done = bf16[768,768]{0,1:T(8,128)(2,1)} async-done(((bf16[768,96]{0,1:T(8,128)(2,1)}), bf16[768,768]{0,1:T(8,128)(2,1)}) %all-gather.9.cloned.1.call-update) | async-done | bytes 1179664 | tf_op jit(solution)/shard_map/all_gather | solution.py:114
  241.2 16.5 %convolution_convert_fusion.2 = bf16[1536,768]{1,0:T(8,128)(2,1)} fusion(bf16[768,768]{0,1:T(8,128)(2,1)} %all-gather.9.cloned.1.call-done, bf16[1536,768]{1,0:T(8,128)(2,1)} %fusion.110, bf16[768,768]{1,0:T(8,128)(2,1)} %all-gather.7.cloned.1.call-done, f32[768]{0:T(1024)S(1)} %copy-done.36), kind=kOutput, calls=%fused_computation.153 | convolution fusion | flops 3702915072 | bytes 7080960 | tf_op jit(solution)/shard_map/dot_general | solution.py:150
  258.3 6.8 all-gather.11.cloned.1.call-done
  265.1 3.2 convert_reduce_fusion
  268.3 4.5 copy.120
  272.8 39.2 %all-reduce.9.cloned.1.call-done = bf16[1536,768]{1,0:T(8,128)(2,1)} async-done(((bf16[1536,768]{1,0:T(8,128)(2,1)}), bf16[1536,768]{1,0:T(8,128)(2,1)}) %all-reduce.9.cloned.1.call-update) | async-done | bytes 2359312 | tf_op jit(solution)/shard_map/psum | solution.py:34
  312.1 4.6 fusion.125
  316.7 2.7 multiply_reduce_fusion.5
  319.4 4.4 fusion.97
  323.8 2.9 fusion.161
  330.4 14.0 %fusion.159 = (f32[768]{0:T(1024)S(1)}, bf16[1536,768]{1,0:T(8,128)(2,1)S(1)}, f32[1536,768]{1,0:T(8,128)}) fusion(f32[1536,768]{1,0:T(8,128)S(1)} %fusion.171, f32[768]{0:T(1024)S(1)} %copy-done.36, bf16[1536,768]{1,0:T(8,128)(2,1)S(1)} %get-tuple-element.432, bf16[768,768]{0,1:T(8,128)(2,1)S(1)} %copy-done.35), kind=kOutput, calls=%fused_computation.235 | convolution fusion | flops 1899232512 | bytes 15341568 | tf_op jit(solution)/shard_map/dot_general | solution.py:171
  345.8 3.5 convolution_convert_fusion.1
  349.6 3.4 fusion.170
  352.9 6.7 reshape.265
  359.7 3.0 add_convert_fusion
  366.3 38.8 %all-reduce.11.cloned.1.call-done = bf16[1536,768]{1,0:T(8,128)(2,1)} async-done(((bf16[1536,768]{1,0:T(8,128)(2,1)}), bf16[1536,768]{1,0:T(8,128)(2,1)}) %all-reduce.11.cloned.1.call-update) | async-done | bytes 2359312 | tf_op jit(solution)/shard_map/psum | solution.py:34
  405.1 5.8 multiply_reduce_fusion.1
  411.1 4.6 fusion.158
  422.8 46.1 %while.41 = (s32[]{:T(128)}, f32[3,512,3,64]{1,3,2,0:T(8,128)}, bf16[3,512,3,64]{1,3,2,0:T(8,128)(2,1)}, f32[3,512,3,64]{1,3,2,0:T(8,128)}, bf16[3,3,512,512]{3,...) while((s32[]{:T(128)}, f32[3,512,3,64]{1,3,2,0:T(8,128)}, ...), condition=%wide.region_17.18_spmd, body=%wide.region_15.17_spmd.sunk | while | flops 512424448 | bytes 34580112 | solution.py:203
  424.4 2.7 fusion.229
  439.8 2.7 fusion.229
  455.1 2.7 fusion.229
  476.2 3.5 fusion.112
  479.8 23.6 %while.42 = (s32[]{:T(128)}, bf16[3,512,3,64]{1,3,2,0:T(8,128)(2,1)S(1)}, bf16[3,512,3,64]{1,3,2,0:T(8,128)(2,1)}, s32[3,512]{1,0:T(4,128)}, bf16[3,512,3,64]{1,...) while((s32[]{:T(128)}, ...), condition=%wide.region_26.27_spmd, body=%wide.region_23.26_spmd.sunk | while | flops 312576512 | bytes 5136481 | solution.py:136
  481.0 3.1 fusion.238
  484.1 3.9 fusion.239
  489.0 3.2 fusion.238
  492.1 3.5 fusion.239
  496.6 3.3 fusion.238
  499.9 3.5 fusion.239
  504.1 5.3 fusion.121
  509.4 7.4 fusion.113
  519.2 2.7 fusion.172
  527.0 39.7 %all-reduce = (f32[2,192]{1,0:T(2,128)}, f32[768]{0:T(1024)}, f32[1,768]{1,0:T(1,128)S(1)}, f32[1,768]{1,0:T(1,128)S(1)}, f32[1,768]{1,0:T(1,128)S(1)}, /*index=...) all-reduce(f32[2,192]{1,0:T(2,128)S(1)} %pad_maximum_fusion.5, ...), channel_id=1, replica_groups=mesh['dp'=8,'tensor'=4] {'dp'}, use_global_device_ids=true, to_apply=%region_22.23 | all-reduce | flops 5760 | bytes 46080 | tf_op jit(solution)/shard_map/psum | solution.py:233
  573.2 184.3 %all-reduce.13.cloned.1.call-done = (f32[768,3,192]{0,2,1:T(8,128)}, f32[192,768]{1,0:T(8,128)}, f32[768,768]{1,0:T(8,128)}, f32[768,768]{1,0:T(8,128)}) async-done(((f32[768,3,192]{0,2,1:T(8,128)}, f32[192,768]{1,0:T(8,128)}, f32[768,768]{1,0:T(8,128)}, f32[768,768]{1,0:T(8,128)}), (f32[768,3,192]{0,2,1:T(8,128)}, f32[192,768]{1,0:T(8,128)}, f32[768,768]{1,0:T(8,128)}, ...) | async-done | bytes 7077904 | tf_op jit(solution)/shard_map/psum | solution.py:233
  757.5 2.9 copy.203
  (235 shorter events, 139.0 us)
Async XLA Ops:
  8.0 82.7 %all-gather.5.cloned.1.call-start = ((), (), s32[]{:S(2)}) async-start(), calls=%async_computation.1 | async-start | bytes 2949120 | tf_op jit(solution)/shard_map/all_gather | solution.py:103
  8.7 200.9 %all-reduce.7.cloned.1.call-start = ((), (), s32[]{:S(2)}) async-start(), calls=%async_computation.2 | async-start | bytes 4718592 | tf_op jit(solution)/shard_map/psum | solution.py:34
  50.6 43.0 %copy-start.20 = (bf16[768,3,192]{0,2,1:T(8,128)(2,1)}, bf16[768,3,192]{0,2,1:T(8,128)(2,1)S(1)}, u32[]{:S(2)}) copy-start(bf16[768,3,192]{0,2,1:T(8,128)(2,1)S(1)} %copy.113) | copy-start | bytes 2654212
  50.6 40.0 %copy-start.33 = (f32[2,192]{1,0:T(2,128)S(1)}, f32[2,192]{1,0:T(2,128)}, u32[]{:S(2)}) copy-start(f32[2,192]{1,0:T(2,128)} %param.24) | copy-start | bytes 4612
  90.7 5.7 copy-start.27
  93.6 317.4 %copy-start = (bf16[3,512,768]{2,1,0:T(8,128)(2,1)}, bf16[3,512,768]{2,1,0:T(8,128)(2,1)S(1)}, u32[]{:S(2)}) copy-start(bf16[3,512,768]{2,1,0:T(8,128)(2,1)S(1)} %copy.111) | copy-start | bytes 7077892
  149.4 5.2 copy-start.23
  149.4 5.9 copy-start.24
  151.1 5.8 copy-start.30
  151.1 5.9 copy-start.31
  151.1 5.9 copy-start.32
  154.6 61.8 %all-gather.7.cloned.1.call-start = ((), (), s32[]{:S(2)}) async-start(), calls=%async_computation.3 | async-start | bytes 1327104 | tf_op jit(solution)/shard_map/all_gather | solution.py:110
  155.3 85.9 %all-gather.9.cloned.1.call-start = ((), (), s32[]{:S(2)}) async-start(), calls=%async_computation.4 | async-start | bytes 1327104 | tf_op jit(solution)/shard_map/all_gather | solution.py:114
  156.1 109.0 %all-gather.11.cloned.1.call-start = ((), (), s32[]{:S(2)}) async-start(), calls=%async_computation.6 | async-start | bytes 2949120 | tf_op jit(solution)/shard_map/all_gather | solution.py:104
  156.7 155.4 %all-reduce.9.cloned.1.call-start = ((), (), s32[]{:S(2)}) async-start(), calls=%async_computation.5 | async-start | bytes 4718592 | tf_op jit(solution)/shard_map/psum | solution.py:34
  157.0 166.8 %copy-start.25 = (f32[768]{0:T(1024)}, f32[768]{0:T(1024)S(1)}, u32[]{:S(2)}) copy-start(f32[768]{0:T(1024)S(1)} %get-tuple-element.353) | copy-start | bytes 9220
  209.7 2.7 copy-start.2
  213.6 27.6 %copy-start.36 = (f32[768]{0:T(1024)S(1)}, f32[768]{0:T(1024)}, u32[]{:S(2)}) copy-start(f32[768]{0:T(1024)} %param.27) | copy-start | bytes 9220
  257.8 147.4 %all-reduce.11.cloned.1.call-start = ((), (), s32[]{:S(2)}) async-start(), calls=%async_computation.7 | async-start | bytes 4718592 | tf_op jit(solution)/shard_map/psum | solution.py:34
  312.1 4.6 copy-start.3
  312.1 4.6 copy-start.8
  316.6 2.8 copy-start.6
  323.8 4.3 copy-start.7
  323.8 4.3 copy-start.9
  323.8 4.5 copy-start.34
  328.1 2.2 copy-start.13
  328.3 2.0 copy-start.35
  330.4 14.0 %copy-start.37 = (f32[1536,768]{1,0:T(8,128)}, f32[1536,768]{1,0:T(8,128)S(1)}, u32[]{:S(2)}) copy-start(f32[1536,768]{1,0:T(8,128)S(1)} %fusion.171) | copy-start | bytes 14155780
  344.3 1.4 copy-start.15
  345.8 3.7 copy-start.28
  345.8 3.8 copy-start.21
  349.2 219.3 %reduce-scatter.4.cloned.1.call-start = ((), (), s32[]{:S(2)}) async-start(), calls=%async_computation.8 | async-start | bytes 2949120
  405.1 5.9 copy-start.4
  405.1 5.9 copy-start.11
  411.1 6.8 copy-start.12
  415.7 2.2 copy-start.5
  472.8 3.4 copy-start.22
  479.6 277.8 %all-reduce.13.cloned.1.call-start = ((), (), s32[]{:S(2)}) async-start(), calls=%async_computation.9 | async-start | bytes 14155776 | tf_op jit(solution)/shard_map/psum | solution.py:233
  479.8 24.3 %copy-start.10 = (bf16[1536,768]{1,0:T(8,128)(2,1)S(1)}, bf16[1536,768]{1,0:T(8,128)(2,1)}, u32[]{:S(2)}) copy-start(bf16[1536,768]{1,0:T(8,128)(2,1)} %fusion.110) | copy-start | bytes 7077892
  503.4 6.0 copy-start.14
  504.1 12.7 %slice-start = ((s8[4718592]{0:T(1024)(128)(4,1)}), s8[4194304]{0:T(1024)(128)(4,1)S(1)}, s32[]{:S(2)}) async-start(s8[4718592]{0:T(1024)(128)(4,1)} %bitcast.304), calls=%async_computation.10 | async-start | bytes 8388608
  509.4 7.4 slice-start.1
  516.8 1.8 copy-start.1
  516.8 2.4 copy-start.19
  522.0 1.6 copy-start.26
  522.0 1.6 copy-start.29
  757.5 4.9 copy-start.17
  757.5 6.3 copy-start.16
  (1 other events, 1.2 us)
Sparse Core Ops, SparseCore 0:
  10.4 26.7 all-gather.4
  154.7 54.9 all-reduce.6
  257.9 54.1 all-reduce.8
  349.4 55.7 all-reduce.10
  479.8 33.1 reduce-scatter.3
Sparse Core Ops, SparseCore 1:
  157.8 40.7 all-gather.6
  201.2 40.0 all-gather.8
  242.6 22.4 all-gather.10
  522.1 235.4 all-reduce.12
where the time goes:
time: 782 us; the launch traced here: 773 us
  waiting for transfers between devices  347 us (44%)
  matrix products  135 us (17%)
  blocking collectives  112 us (14%)
  local copies, waits for them, and re-layouts  99 us (13%)
  other arithmetic  61.8 us (8%)
  between operations  16.5 us (2%)
    psum x1, waiting for transfers between devices, body(): lax.psum((grad_qkv, grad_b_qv, grad_out, grad_bias_out, grad_gain_one, gr...  184 us
    psum x3, waiting for transfers between devices, branch_total(): lax.psum(partial_value.astype(jnp.bfloat16), 'tensor').astype(jnp.float32)  130 us
    psum x1, blocking collectives, body(): lax.psum((grad_qkv, grad_b_qv, grad_out, grad_bias_out, grad_gain_one, gr...  39.7 us
    all_gather x1, blocking collectives, body(): lax.all_gather(w_qkv.astype(jnp.bfloat16), 'dp', axis=0, tiled=True)  38.8 us
    all_gather x1, blocking collectives, body(): lax.all_gather(w_out.astype(jnp.bfloat16), 'dp', axis=1, tiled=True)  33 us
    all_gather x1, waiting for transfers between devices, body(): lax.all_gather(w_down.astype(jnp.bfloat16), 'dp', axis=1, tiled=True)  24.9 us
    dynamic_update_slice x12, local copies, waits for them, and re-layouts, attend_all(): lax.map(one_row, (packed[:, :, 0], packed[:, :, 1], packed[:, :, 2], prev...  21.5 us
    unnamed x91, local copies, waits for them, and re-layouts  20.5 us
  transfers between devices with their start and end apart: 9, of which 6 were waited for; matrix products, arithmetic and copies ran while one was open for 15% of the time, Pallas kernels for 0%

commit v1 on v0

--- a/solution.py
+++ b/solution.py
@@ -31,7 +31,9 @@
 
 
 def branch_total(partial_value):
-    return lax.psum(partial_value.astype(jnp.bfloat16), "tensor").astype(jnp.float32)
+    return jnp.sum(lax.all_gather(partial_value.astype(jnp.bfloat16), "tensor"), axis=0).astype(
+        jnp.float32
+    )
 
 
 def attend_rows(query, keys, values, previous, segment, inv_root):

time: 782 us -> 896 us (1.15)
  waiting for transfers between devices: 347 us -> 429 us
  other arithmetic: 61.8 us -> 104 us
  local copies, waits for them, and re-layouts: 99 us -> 89.1 us
    all_gather x0 -> x3, waiting for transfers between devices: none -> 168 us  [branch_total(): lax.all_gather(partial_value.astype(jnp.bfloat16), 'tensor')]
    psum x3 -> x0, waiting for transfers between devices: 130 us -> none  [branch_total(): lax.psum(partial_value.astype(jnp.bfloat16), 'tensor').astype(jnp.float32)]
    all_gather x1, waiting for transfers between devices: 0.01 us -> 42.5 us  [body(): lax.all_gather(w_up.astype(jnp.bfloat16), 'dp', axis=0, tiled=True)]
    reduce_sum x2 -> x4, other arithmetic: 7.79 us -> 26.3 us  [the longest x3 21.5 us: branch_total(): jnp.sum(lax.all_gather(partial_value.astype(jnp.bfloat16), 'tensor'), axi...]
    convert_element_type x1, other arithmetic: 2.86 us -> 14.8 us  [body(): grad_sum_two_bf = grad_sum_two.astype(jnp.bfloat16)]
    dynamic_update_slice x12, local copies, waits for them, and re-layouts: 21.5 us -> 11.7 us  [attend_all(): lax.map(one_row, (packed[:, :, 0], packed[:, :, 1], packed[:, :, 2], prev...]
    unnamed x91 -> x139, local copies, waits for them, and re-layouts: 20.5 us -> 17.9 us
  transfers between devices with their start and end apart: 9 -> 9, of which waited for: 6 -> 7; matrix products, arithmetic and copies ran while one was open for 15% -> 14% of each run, Pallas kernels for 0% -> 0%
where the time goes in v1:
time: 896 us; the launch traced here: 887 us
  waiting for transfers between devices  429 us (48%)
  matrix products  138 us (15%)
  blocking collectives  110 us (12%)
  other arithmetic  104 us (12%)
  local copies, waits for them, and re-layouts  89.1 us (10%)
  between operations  15.2 us (2%)
    psum x1, waiting for transfers between devices, body(): lax.psum((grad_qkv, grad_b_qv, grad_out, grad_bias_out, grad_gain_one, gr...  185 us
    all_gather x3, waiting for transfers between devices, branch_total(): lax.all_gather(partial_value.astype(jnp.bfloat16), 'tensor')  168 us
    all_gather x1, waiting for transfers between devices, body(): lax.all_gather(w_up.astype(jnp.bfloat16), 'dp', axis=0, tiled=True)  42.5 us
    psum x1, blocking collectives, body(): lax.psum((grad_qkv, grad_b_qv, grad_out, grad_bias_out, grad_gain_one, gr...  40.1 us
    all_gather x1, blocking collectives, body(): lax.all_gather(w_qkv.astype(jnp.bfloat16), 'dp', axis=0, tiled=True)  38.8 us
    all_gather x1, blocking collectives, body(): lax.all_gather(w_out.astype(jnp.bfloat16), 'dp', axis=1, tiled=True)  31.2 us
    all_gather x1, waiting for transfers between devices, body(): lax.all_gather(w_down.astype(jnp.bfloat16), 'dp', axis=1, tiled=True)  25.1 us
    reduce_sum x3, other arithmetic, branch_total(): jnp.sum(lax.all_gather(partial_value.astype(jnp.bfloat16), 'tensor'), axi...  21.5 us
  transfers between devices with their start and end apart: 9, of which 7 were waited for; matrix products, arithmetic and copies ran while one was open for 14% of the time, Pallas kernels for 0%

profile of v1, /device:TPU:0, one launch (start us, length us, event | category | flops | bytes accessed | tf_op | source)
XLA Modules:
  0.0 887.0 jit_solution(12806196466580323640)
XLA Ops:
  9.1 38.8 %all_gather.37 = bf16[768,3,192]{2,1,0:T(4,128)(2,1)S(1)} all-gather(bf16[96,3,192]{2,1,0:T(4,128)(2,1)S(1)} %copy.116), channel_id=1, replica_groups=mesh['dp'=8,'tensor'=4] {'dp'}, dimensions={0}, use_global_device_ids=true | all-gather | bytes 995328 | tf_op jit(solution)/shard_map/all_gather | solution.py:111
  50.0 6.7 copy.121
  56.8 31.2 %all_gather.38 = bf16[192,768]{0,1:T(8,128)(2,1)S(1)} all-gather(bf16[192,96]{0,1:T(8,128)(2,1)S(1)} %copy.123), channel_id=1, replica_groups=mesh['dp'=8,'tensor'=4] {'dp'}, dimensions={1}, use_global_device_ids=true | all-gather | bytes 331776 | tf_op jit(solution)/shard_map/all_gather | solution.py:115
  88.1 2.8 copy.115
  90.9 4.6 add_convert_fusion.1
  95.5 5.2 reshape.983
  109.7 28.1 %while.40 = (s32[]{:T(128)}, bf16[3,512,3,64]{1,3,2,0:T(8,128)(2,1)}, bf16[3,3,512,512]{3,2,1,0:T(8,128)(2,1)}, f32[3,3,512]{2,1,0:T(4,128)}, bf16[3,512,3,64]{1...) while((s32[]{:T(128)}, ...), condition=%wide.region_3.4_spmd, body=%wide.region_0.3_spmd.sunk | while | flops 211909120 | bytes 20769400 | solution.py:138
  144.9 60.2 %all-gather.19.cloned.1.call-done = bf16[6144,768]{1,0:T(8,128)(2,1)} async-done(((bf16[1536,768]{1,0:T(8,128)(2,1)}), bf16[6144,768]{1,0:T(8,128)(2,1)}) %all-gather.19.cloned.1.call-update) | async-done | bytes 9437200 | tf_op jit(solution)/shard_map/all_gather | solution.py:34
  205.1 7.3 reduce_sum.216
  212.4 4.5 fusion.164
  217.0 3.0 multiply_reduce_fusion.6
  220.0 3.9 fusion.112
  223.9 25.1 %all-gather.15.cloned.1.call-done = bf16[768,768]{0,1:T(8,128)(2,1)} async-done(((bf16[768,96]{0,1:T(8,128)(2,1)}), bf16[768,768]{0,1:T(8,128)(2,1)}) %all-gather.15.cloned.1.call-update) | async-done | bytes 1179664 | tf_op jit(solution)/shard_map/all_gather | solution.py:116
  249.0 42.5 %all-gather.13.cloned.1.call-done = bf16[768,768]{1,0:T(8,128)(2,1)} async-done(((bf16[96,768]{1,0:T(8,128)(2,1)}), bf16[768,768]{1,0:T(8,128)(2,1)}) %all-gather.13.cloned.1.call-update) | async-done | bytes 1179664 | tf_op jit(solution)/shard_map/all_gather | solution.py:112
  291.4 16.5 %convolution_convert_fusion.2 = bf16[1536,768]{1,0:T(8,128)(2,1)} fusion(bf16[768,768]{0,1:T(8,128)(2,1)} %all-gather.15.cloned.1.call-done, bf16[1536,768]{1,0:T(8,128)(2,1)} %fusion.112, bf16[768,768]{1,0:T(8,128)(2,1)} %all-gather.13.cloned.1.call-done, f32[768]{0:T(1024)S(1)} %copy-done.57), kind=kOutput, calls=%fused_computation.157 | convolution fusion | flops 3702915072 | bytes 7080960 | tf_op jit(solution)/shard_map/dot_general | solution.py:152
  308.4 7.3 all-gather.17.cloned.1.call-done
  315.7 4.3 copy.125
  320.0 62.0 %all-gather.21.cloned.1.call-done = bf16[6144,768]{1,0:T(8,128)(2,1)} async-done(((bf16[1536,768]{1,0:T(8,128)(2,1)}), bf16[6144,768]{1,0:T(8,128)(2,1)}) %all-gather.21.cloned.1.call-update) | async-done | bytes 9437200 | tf_op jit(solution)/shard_map/all_gather | solution.py:34
  382.0 7.1 reduce_sum.219
  389.1 5.3 fusion.163
  394.4 3.0 multiply_reduce_fusion.5
  397.4 4.8 multiply_reduce_fusion.8
  402.9 14.8 %fusion.159 = (bf16[1536,768]{1,0:T(8,128)(2,1)S(1)}, f32[1536,768]{1,0:T(8,128)}) fusion(f32[1536]{0:T(1024)S(1)} %rsqrt.27, f32[1536]{0:T(1024)S(1)} %div.61, f32[1536]{0:T(1024)S(1)} %div.59, f32[768]{0:T(1024)S(1)} %get-tuple-element.354, bf16[3,512,768]{2,1,0:T(8,128)(2,1)} %copy.125, f32[1536]{0:T(1024)S(1)} %div.56, f32[768]{0:T(1024)S(1)} %get-tuple-element.358, ...), kind=kLoop, calls=%fused_computation.237 | loop fusion | flops 23592960 | bytes 16567296 | tf_op jit(solution)/shard_map/convert_element_type | solution.py:165
  419.9 14.7 %fusion.160 = (f32[768]{0:T(1024)}, bf16[1536,768]{1,0:T(8,128)(2,1)S(1)}, f32[1536,768]{1,0:T(8,128)}) fusion(f32[1536,768]{1,0:T(8,128)S(1)} %fusion.174, f32[768]{0:T(1024)S(1)} %copy-done.57, bf16[1536,768]{1,0:T(8,128)(2,1)S(1)} %get-tuple-element.432, bf16[768,768]{0,1:T(8,128)(2,1)S(1)} %copy-done.55), kind=kOutput, calls=%fused_computation.238 | convolution fusion | flops 1899232512 | bytes 15341568 | tf_op jit(solution)/shard_map/dot_general | solution.py:173
  436.1 3.4 convolution_convert_fusion.1
  439.7 4.5 fusion.173
  444.2 6.9 reshape.985
  451.1 3.5 add_convert_fusion
  458.3 45.6 %all-gather.23.cloned.1.call-done = bf16[6144,768]{1,0:T(8,128)(2,1)} async-done(((bf16[1536,768]{1,0:T(8,128)(2,1)}), bf16[6144,768]{1,0:T(8,128)(2,1)}) %all-gather.23.cloned.1.call-update) | async-done | bytes 9437200 | tf_op jit(solution)/shard_map/all_gather | solution.py:34
  504.0 7.1 reduce_sum.224
  511.2 10.1 %multiply_reduce_fusion.1 = (f32[768]{0:T(1024)}, f32[768]{0:T(1024)}, f32[3,512]{1,0:T(4,128)S(1)}, f32[3,512]{1,0:T(4,128)S(1)}, f32[3,512,768]{2,1,0:T(8,128)}) fusion(bf16[3,512,768]{2,1,0:T(8,128)(2,1)} %copy.125, f32[3,512,768]{2,1,0:T(8,128)} %get-tuple-element.435, f32[3,512]{1,0:T(4,128)S(1)} %copy-done.27, ...), kind=kLoop, calls=%fused_computation.103 | loop fusion | flops 22408704 | bytes 18935808 | tf_op jit(solution)/shard_map/reduce_sum | solution.py:161
  521.4 6.4 subtract_multiply_fusion.1
  535.0 46.3 %while.41 = (s32[]{:T(128)}, f32[3,512,3,64]{1,3,2,0:T(8,128)}, bf16[3,512,3,64]{1,3,2,0:T(8,128)(2,1)}, f32[3,512,3,64]{1,3,2,0:T(8,128)}, bf16[3,3,512,512]{3,...) while((s32[]{:T(128)}, f32[3,512,3,64]{1,3,2,0:T(8,128)}, ...), condition=%wide.region_17.18_spmd, body=%wide.region_15.17_spmd.sunk | while | flops 512424448 | bytes 34580112 | solution.py:205
  536.8 2.7 fusion.234
  588.6 3.5 fusion.113
  592.2 23.6 %while.42 = (s32[]{:T(128)}, bf16[3,512,3,64]{1,3,2,0:T(8,128)(2,1)S(1)}, bf16[3,512,3,64]{1,3,2,0:T(8,128)(2,1)}, s32[3,512]{1,0:T(4,128)}, bf16[3,512,3,64]{1,...) while((s32[]{:T(128)}, ...), condition=%wide.region_26.27_spmd, body=%wide.region_23.26_spmd.sunk | while | flops 312576512 | bytes 5136481 | solution.py:138
  593.5 3.1 fusion.243
  596.6 3.9 fusion.244
  601.4 3.2 fusion.243
  604.6 3.5 fusion.244
  609.1 3.2 fusion.243
  612.3 3.5 fusion.244
  616.6 5.3 fusion.122
  621.9 7.4 fusion.114
  632.9 2.7 fusion.175
  640.7 40.1 %all-reduce = (f32[2,192]{1,0:T(2,128)}, f32[768]{0:T(1024)}, f32[1,768]{1,0:T(1,128)S(1)}, f32[1,768]{1,0:T(1,128)S(1)}, f32[1,768]{1,0:T(1,128)S(1)}, /*index=...) all-reduce(f32[2,192]{1,0:T(2,128)S(1)} %pad_maximum_fusion.5, ...), channel_id=1, replica_groups=mesh['dp'=8,'tensor'=4] {'dp'}, use_global_device_ids=true, to_apply=%region_22.23 | all-reduce | flops 5760 | bytes 46080 | tf_op jit(solution)/shard_map/psum | solution.py:235
  687.4 185.0 %all-reduce.4.cloned.1.call-done = (f32[768,3,192]{0,2,1:T(8,128)}, f32[192,768]{1,0:T(8,128)}, f32[768,768]{1,0:T(8,128)}, f32[768,768]{1,0:T(8,128)}) async-done(((f32[768,3,192]{0,2,1:T(8,128)}, f32[192,768]{1,0:T(8,128)}, f32[768,768]{1,0:T(8,128)}, f32[768,768]{1,0:T(8,128)}), (f32[768,3,192]{0,2,1:T(8,128)}, f32[192,768]{1,0:T(8,128)}, f32[768,768]{1,0:T(8,128)}, ...) | async-done | bytes 7077904 | tf_op jit(solution)/shard_map/psum | solution.py:235
  872.4 2.9 copy.211
  (294 shorter events, 137.9 us)
Async XLA Ops:
  7.2 80.9 %all-gather.11.cloned.1.call-start = ((), (), s32[]{:S(2)}) async-start(), calls=%async_computation.1 | async-start | bytes 2949120 | tf_op jit(solution)/shard_map/all_gather | solution.py:105
  7.9 197.2 %all-gather.19.cloned.1.call-start = ((), (), s32[]{:S(2)}) async-start(), calls=%async_computation.5 | async-start | bytes 11796480 | tf_op jit(solution)/shard_map/all_gather | solution.py:34
  50.0 6.7 copy-start.32
  50.0 38.0 %copy-start.54 = (f32[2,192]{1,0:T(2,128)S(1)}, f32[2,192]{1,0:T(2,128)}, u32[]{:S(2)}) copy-start(f32[2,192]{1,0:T(2,128)} %param.24) | copy-start | bytes 4612
  88.1 7.4 copy-start.46
  141.8 107.1 %all-gather.15.cloned.1.call-start = ((), (), s32[]{:S(2)}) async-start(), calls=%async_computation.3 | async-start | bytes 1327104 | tf_op jit(solution)/shard_map/all_gather | solution.py:116
  142.6 148.8 %all-gather.13.cloned.1.call-start = ((), (), s32[]{:S(2)}) async-start(), calls=%async_computation.2 | async-start | bytes 1327104 | tf_op jit(solution)/shard_map/all_gather | solution.py:112
  143.3 172.4 %all-gather.17.cloned.1.call-start = ((), (), s32[]{:S(2)}) async-start(), calls=%async_computation.4 | async-start | bytes 2949120 | tf_op jit(solution)/shard_map/all_gather | solution.py:106
  143.9 238.0 %all-gather.21.cloned.1.call-start = ((), (), s32[]{:S(2)}) async-start(), calls=%async_computation.6 | async-start | bytes 11796480 | tf_op jit(solution)/shard_map/all_gather | solution.py:34
  144.2 258.6 %copy-start.30 = (f32[768]{0:T(1024)}, f32[768]{0:T(1024)S(1)}, u32[]{:S(2)}) copy-start(f32[768]{0:T(1024)S(1)} %get-tuple-element.359) | copy-start | bytes 9220
  144.9 257.9 %copy-start.19 = (f32[768]{0:T(1024)}, f32[768]{0:T(1024)S(1)}, u32[]{:S(2)}) copy-start(f32[768]{0:T(1024)S(1)} %get-tuple-element.355) | copy-start | bytes 9220
  144.9 257.9 %copy-start.28 = (f32[768]{0:T(1024)}, f32[768]{0:T(1024)S(1)}, u32[]{:S(2)}) copy-start(f32[768]{0:T(1024)S(1)} %get-tuple-element.354) | copy-start | bytes 9220
  205.1 7.3 copy-start.1
  217.0 185.9 %copy-start.22 = (f32[1536]{0:T(1024)}, f32[1536]{0:T(1024)S(1)}, u32[]{:S(2)}) copy-start(f32[1536]{0:T(1024)S(1)} %div.53) | copy-start | bytes 18436
  219.9 71.5 %copy-start.57 = (f32[768]{0:T(1024)S(1)}, f32[768]{0:T(1024)}, u32[]{:S(2)}) copy-start(f32[768]{0:T(1024)} %param.27) | copy-start | bytes 9220
  219.9 169.1 %copy-start.16 = (f32[3,512]{1,0:T(4,128)}, f32[3,512]{1,0:T(4,128)S(1)}, u32[]{:S(2)}) copy-start(f32[3,512]{1,0:T(4,128)S(1)} %add_rsqrt_fusion.1) | copy-start | bytes 18436
  220.0 182.9 %copy-start.24 = (f32[1536]{0:T(1024)}, f32[1536]{0:T(1024)S(1)}, u32[]{:S(2)}) copy-start(f32[1536]{0:T(1024)S(1)} %rsqrt.25) | copy-start | bytes 18436
  308.0 195.9 %all-gather.23.cloned.1.call-start = ((), (), s32[]{:S(2)}) async-start(), calls=%async_computation.7 | async-start | bytes 11796480 | tf_op jit(solution)/shard_map/all_gather | solution.py:34
  397.4 20.4 %copy-start.26 = (f32[3,512]{1,0:T(4,128)}, f32[3,512]{1,0:T(4,128)S(1)}, u32[]{:S(2)}) copy-start(f32[3,512]{1,0:T(4,128)S(1)} %add_rsqrt_fusion) | copy-start | bytes 18436
  397.4 20.4 %copy-start.33 = (f32[1536]{0:T(1024)}, f32[1536]{0:T(1024)S(1)}, u32[]{:S(2)}) copy-start(f32[1536]{0:T(1024)S(1)} %rsqrt.27) | copy-start | bytes 18436
  402.2 15.5 %copy-start.35 = (f32[1536]{0:T(1024)}, f32[1536]{0:T(1024)S(1)}, u32[]{:S(2)}) copy-start(f32[1536]{0:T(1024)S(1)} %div.61) | copy-start | bytes 18436
  402.8 15.0 %copy-start.41 = (f32[3,512]{1,0:T(4,128)}, f32[3,512]{1,0:T(4,128)S(1)}, u32[]{:S(2)}) copy-start(f32[3,512]{1,0:T(4,128)S(1)} %broadcast_multiply_fusion.3) | copy-start | bytes 18436
  402.9 14.9 %copy-start.37 = (f32[1536]{0:T(1024)}, f32[1536]{0:T(1024)S(1)}, u32[]{:S(2)}) copy-start(f32[1536]{0:T(1024)S(1)} %div.59) | copy-start | bytes 18436
  402.9 14.9 %copy-start.4 = (bf16[1536,768]{1,0:T(8,128)(2,1)S(1)}, bf16[1536,768]{1,0:T(8,128)(2,1)}, u32[]{:S(2)}) copy-start(bf16[1536,768]{1,0:T(8,128)(2,1)} %fusion.112) | copy-start | bytes 7077892
  402.9 14.9 %copy-start.56 = (bf16[768,768]{1,0:T(8,128)(2,1)S(1)}, bf16[768,768]{1,0:T(8,128)(2,1)}, u32[]{:S(2)}) copy-start(bf16[768,768]{1,0:T(8,128)(2,1)} %all-gather.13.cloned.1.call-done) | copy-start | bytes 3538948
  419.9 14.7 %copy-start.59 = (f32[1536,768]{1,0:T(8,128)}, f32[1536,768]{1,0:T(8,128)S(1)}, u32[]{:S(2)}) copy-start(f32[1536,768]{1,0:T(8,128)S(1)} %fusion.174) | copy-start | bytes 14155780
  439.5 243.1 %reduce-scatter.4.cloned.1.call-start = ((), (), s32[]{:S(2)}) async-start(), calls=%async_computation.8 | async-start | bytes 2949120
  503.9 7.1 copy-start.17
  503.9 7.1 copy-start.20
  503.9 7.1 copy-start.27
  503.9 7.1 copy-start.29
  503.9 7.1 copy-start.40
  504.0 7.2 copy-start.42
  511.1 10.2 %copy-start.23 = (f32[1536]{0:T(1024)S(1)}, f32[1536]{0:T(1024)}, u32[]{:S(2)}) copy-start(f32[1536]{0:T(1024)} %copy-done.22) | copy-start | bytes 18436
  511.1 10.2 %copy-start.25 = (f32[1536]{0:T(1024)S(1)}, f32[1536]{0:T(1024)}, u32[]{:S(2)}) copy-start(f32[1536]{0:T(1024)} %copy-done.24) | copy-start | bytes 18436
  511.1 10.2 %copy-start.31 = (f32[768]{0:T(1024)S(1)}, f32[768]{0:T(1024)}, u32[]{:S(2)}) copy-start(f32[768]{0:T(1024)} %copy-done.30) | copy-start | bytes 9220
  511.1 10.2 %copy-start.34 = (f32[1536]{0:T(1024)S(1)}, f32[1536]{0:T(1024)}, u32[]{:S(2)}) copy-start(f32[1536]{0:T(1024)} %copy-done.33) | copy-start | bytes 18436
  511.2 10.2 %copy-start.36 = (f32[1536]{0:T(1024)S(1)}, f32[1536]{0:T(1024)}, u32[]{:S(2)}) copy-start(f32[1536]{0:T(1024)} %copy-done.35) | copy-start | bytes 18436
  511.2 10.2 %copy-start.38 = (f32[1536]{0:T(1024)S(1)}, f32[1536]{0:T(1024)}, u32[]{:S(2)}) copy-start(f32[1536]{0:T(1024)} %copy-done.37) | copy-start | bytes 18436
  592.1 280.3 %all-reduce.4.cloned.1.call-start = ((), (), s32[]{:S(2)}) async-start(), calls=%async_computation.9 | async-start | bytes 14155776 | tf_op jit(solution)/shard_map/psum | solution.py:235
  592.2 24.3 %copy-start.5 = (bf16[1536,768]{1,0:T(8,128)(2,1)S(1)}, bf16[1536,768]{1,0:T(8,128)(2,1)}, u32[]{:S(2)}) copy-start(bf16[1536,768]{1,0:T(8,128)(2,1)} %fusion.112) | copy-start | bytes 7077892
  616.5 12.8 %slice-start = ((s8[4718592]{0:T(1024)(128)(4,1)}), s8[4194304]{0:T(1024)(128)(4,1)S(1)}, s32[]{:S(2)}) async-start(s8[4718592]{0:T(1024)(128)(4,1)} %bitcast.303), calls=%async_computation.10 | async-start | bytes 8388608
  616.5 12.7 %slice-start.2 = ((s8[4718592]{0:T(1024)(128)(4,1)}), s8[4194304]{0:T(1024)(128)(4,1)S(1)}, s32[]{:S(2)}) async-start(s8[4718592]{0:T(1024)(128)(4,1)} %bitcast.311), calls=%async_computation.12 | async-start | bytes 8388608
  621.8 7.5 slice-start.1
  621.8 7.5 slice-start.3
  621.8 7.5 copy-start.18
  621.8 7.5 copy-start.21
  621.8 7.5 copy-start.44
  (25 other events, 101.9 us)
Sparse Core Ops, SparseCore 0:
  9.6 26.7 all-gather.10
  141.9 63.1 all-gather.18
  207.9 41.0 all-gather.14
  251.6 39.8 all-gather.12
  292.8 22.8 all-gather.16
  317.7 64.2 all-gather.20
  439.7 64.2 all-gather.22
  592.2 33.0 reduce-scatter.3
  635.8 236.5 all-reduce.3
